TPU v7x, 32 devices: a whole 2x2x4 slice. The times are simulated.
32 devices in a mesh: cohort: 2 (over x), region: 16 (over z, y, core).
Axes of the slice: x: 2, y: 2, z: 4, core: 2. Of those that a mesh axis runs over, the one named last changes fastest.
Arguments:
- dosage: bfloat16 [4096, 16384], P('cohort', 'region'), parts along dimension 0, may hold values from 0 to 2, as said below
- eigvec: bfloat16 [16384, 2048], P('region', 'cohort'), parts along dimension 1, may hold values from -1 to 1, as said below
- eigval: float32 [2, 16384], P('cohort', 'region'), parts along dimension 0, may hold values from 64 to 65536
- pheno: bfloat16 [4096, 128], P('cohort'), parts along dimension 0, may hold values from 0 to 1, as said below
Outputs:
- level1_weights: float32 [128, 128], P('region', 'cohort'), parts along dimension 1
There are 2 independent parts, one for each index of `cohort`. A program takes and returns all parts, laid end to end along the dimension named above; each array names one. Nothing has to cross between parts.
Inputs may be any that keep to these rules, and one draw needn't show every extreme that they name: Every entry is a whole dosage 0, 1 or 2. `eigvec`: the rows of each block form an orthonormal basis up to rounding. `pheno`: every entry is 0 or 1.
All inputs are finite; a program needn't handle non-finite values.
Results may differ from a plain program's by a relative error of at most 0.0051.
Values may be sent and summed in bfloat16 or wider, within the bound.
No kernel may reach another device: no remote copies, remote signals or barrier semaphores. Data moves between devices by JAX's collectives and lax.ppermute only.
A program may use at most 64 MiB of HBM per device.

v0:
```python
import jax
import jax.numpy as jnp
from jax import lax
from jax.sharding import PartitionSpec as P

NEWTON = 3
EPSILON = 1e-05
HERITABILITY = (0.01, 0.25, 0.75, 0.99)
LEVEL_ONE = 0.03125


def standardize(values):
    values = values.astype(jnp.float32)
    center = jnp.mean(values, axis=0)
    spread = jnp.sqrt(jnp.mean(jnp.square(values - center), axis=0) + EPSILON)
    return ((values - center) / spread).astype(jnp.bfloat16)


def fit_traits(moved, target, total_samples):
    count_traits = moved.shape[1]
    design = jnp.moveaxis(moved, 1, 0).reshape(count_traits, -1, moved.shape[3])
    predictors = design.shape[1]
    level_ridge = LEVEL_ONE * total_samples
    all_weights = jnp.zeros((count_traits, predictors), jnp.float32)
    own_weights = jnp.zeros((count_traits, predictors), jnp.float32)
    identity = jnp.eye(predictors, dtype=jnp.float32)
    for newton_step in range(NEWTON):
        logits = jnp.einsum(
            "kqn,kq->kn",
            design,
            all_weights.astype(jnp.bfloat16),
            preferred_element_type=jnp.float32,
        )
        prob = jax.nn.sigmoid(logits)
        resid = (target - prob).astype(jnp.bfloat16)
        weighted = (design * (prob * (1.0 - prob))[:, None, :]).astype(jnp.bfloat16)
        gram = jnp.einsum("kqn,kpn->kqp", weighted, design, preferred_element_type=jnp.float32)
        grad = jnp.einsum("kqn,kn->kq", design, resid, preferred_element_type=jnp.float32)
        grad = grad - level_ridge * own_weights
        factor = jnp.linalg.cholesky(gram + level_ridge * identity)
        partial_solve = lax.linalg.triangular_solve(
            factor, grad[:, :, None], left_side=True, lower=True
        )
        update = lax.linalg.triangular_solve(
            factor, partial_solve, left_side=True, lower=True, transpose_a=True
        )
        own_weights = own_weights + update[:, :, 0]
        all_weights = own_weights
    return own_weights


def on_device(dosage, eigvec, eigval, pheno):
    samples, width = dosage.shape
    traits = pheno.shape[1]
    regions = lax.axis_size("region")
    ridges = len(HERITABILITY)
    per_device = traits // regions
    shrink = jnp.array([width * (1.0 - value) / value for value in HERITABILITY], jnp.float32)
    std_trait = standardize(pheno)
    std_geno = standardize(dosage)
    cross = lax.dot_general(
        std_geno, std_trait, (((0,), (0,)), ((), ())), preferred_element_type=jnp.float32
    ).astype(jnp.bfloat16)
    rotated = lax.dot_general(
        eigvec, cross, (((0,), (0,)), ((), ())), preferred_element_type=jnp.float32
    )
    scaled = (rotated[:, None, :] / (eigval[0][:, None, None] + shrink[None, :, None])).astype(
        jnp.bfloat16
    )
    ridge = jnp.dot(
        eigvec, scaled.reshape(width, ridges * traits), preferred_element_type=jnp.float32
    ).astype(jnp.bfloat16)
    position = lax.axis_index("region")
    predicted = lax.dot_general(
        ridge, std_geno, (((0,), (1,)), ((), ())), preferred_element_type=jnp.float32
    ).astype(jnp.bfloat16)
    predicted = predicted.reshape(ridges, traits, 1, samples)
    moved = lax.all_to_all(predicted, "region", split_axis=1, concat_axis=2, tiled=True)
    target = lax.dynamic_slice_in_dim(pheno, position * per_device, per_device, 1)
    weights = fit_traits(moved, target.astype(jnp.float32).T, samples)
    return weights


def solution(mesh):
    return jax.shard_map(
        on_device,
        mesh=mesh,
        in_specs=(
            P("cohort", "region"),
            P("region", "cohort"),
            P("cohort", "region"),
            P("cohort", None),
        ),
        out_specs=P("region", "cohort"),
        check_vma=False,
    )
```

profile of v0, /device:TPU:13, one launch (start us, length us, event | category | flops | bytes accessed | tf_op | source)
XLA Modules:
  0.0 363.7 jit_solution(3730043652886165444)
XLA Ops:
  0.0 0.0 copy-start
  0.0 0.0 copy-start.1
  0.0 3.0 convert_reduce_fusion
  3.1 0.5 copy-done.1
  3.6 1.1 fusion.2
  4.8 0.0 copy-start.5
  4.8 3.2 fusion.3
  8.0 0.0 copy-done.5
  8.0 0.3 convert_reduce_fusion.1
  8.3 0.3 fusion.27
  8.6 0.0 copy-done
  8.6 0.0 copy-start.6
  8.6 0.0 copy-start.7
  8.6 5.0 %convolution_bitcast_fusion = f32[1024,128]{0,1:T(8,128)} fusion(bf16[1024,1024]{1,0:T(8,128)(2,1)S(1)} %copy-done, bf16[2048,1024]{1,0:T(8,128)(2,1)} %fusion.3, bf16[2048,128]{1,0:T(8,128)(2,1)S(1)} %copy-done.5, f32[128]{0:T(128)S(1)} %add_sqrt_fusion.1, f32[128]{0:T(128)S(1)} %broadcast_multiply_fusion.1), kind=kOutput, calls=%fused_computation.25 | convolution fusion | flops 806486016 | bytes 7341056 | tf_op jit(solution)/shard_map/dot_general | solution.py:64
  13.6 1.2 copy.50
  14.9 0.0 copy-done.6
  14.9 0.0 copy-done.7
  14.9 0.2 broadcast_add_fusion
  15.1 4.6 %divide_convert_fusion = bf16[1024,4,128]{2,1,0:T(4,128)(2,1)} fusion(f32[1024,4]{1,0:T(8,128)S(1)} %broadcast_add_fusion, f32[1024,128]{1,0:T(8,128)S(1)} %copy.50), kind=kLoop, calls=%fused_computation.16 | loop fusion | flops 1048576 | bytes 1589248 | tf_op jit(solution)/shard_map/convert_element_type | solution.py:67
  19.7 7.3 %convolution_convert_fusion = bf16[512,2048]{1,0:T(8,128)(2,1)} fusion(bf16[2048,1024]{1,0:T(8,128)(2,1)} %fusion.3, bf16[1024,1024]{1,0:T(8,128)(2,1)S(1)} %copy-done, bf16[128,8,4,128]{3,2,1,0:T(4,128)(2,1)} %bitcast.211), kind=kOutput, calls=%fused_computation.15 | convolution fusion | flops 3222798336 | bytes 9437184 | tf_op jit(solution)/shard_map/dot_general | solution.py:74
  27.0 4.6 %copy.51 = bf16[4,128,1,2048]{3,0,2,1:T(4,128)(2,1)} copy(bf16[4,128,1,2048]{3,1,0,2:T(8,128)(2,1)} %bitcast.210) | data formatting | bytes 4194304 | tf_op jit(solution)/shard_map/reshape | solution.py:77
  31.6 6.7 %all-to-all-start = ((bf16[4,128,1,2048]{3,0,2,1:T(4,128)(2,1)}), bf16[4,128,1,2048]{3,0,2,1:T(4,128)(2,1)}, u32[]{:S(2)}, u32[]{:S(2)}) async-start(bf16[4,128,1,2048]{3,0,2,1:T(4,128)(2,1)} %copy.51), calls=%async_computation | async-start | bytes 4194304 | tf_op jit(solution)/shard_map/all_to_all | solution.py:78
  38.3 0.2 constant_dynamic-slice_fusion
  38.5 0.2 copy.90
  38.7 47.1 %all-to-all-done = bf16[4,128,1,2048]{3,0,2,1:T(4,128)(2,1)} async-done(((bf16[4,128,1,2048]{3,0,2,1:T(4,128)(2,1)}), bf16[4,128,1,2048]{3,0,2,1:T(4,128)(2,1)}, u32[]{:S(2)}, u32[]{:S(2)}) %all-to-all-start) | async-done | bytes 2097184 | tf_op jit(solution)/shard_map/all_to_all | solution.py:78
  85.8 2.8 copy.52
  88.6 0.0 copy-start.2
  88.6 0.4 fusion.76
  89.0 0.9 copy-done.2
  89.9 0.7 fusion.18
  90.7 0.1 copy.54
  90.9 46.9 %custom-call.15 = f32[8,64,64]{2,1,0:T(8,128)S(1)} custom-call(f32[8,64,64]{2,1,0:T(8,128)S(1)} %fusion.50), custom_call_target="Cholesky" | custom-call | tf_op jit(solution)/shard_map/jit(cholesky)/cholesky | solution.py:40
  137.8 0.1 compare_reduce_fusion.2
  137.9 0.1 select_bitcast_fusion.2
  138.1 39.3 %custom-call.17 = f32[8,1,64,64]{2,3,1,0:T(8,128)S(1)} custom-call(f32[8,1,64,64]{3,2,1,0:T(8,128)S(1)} %select_bitcast_fusion.2), custom_call_target="InvertDiagBlocksLowerTriangular" | custom-call | tf_op jit(solution)/shard_map/triangular_solve/custom-call.2 | solution.py:44
  177.4 0.0 copy-start.3
  177.4 2.4 convolution_bitcast_fusion.4
  179.8 0.4 convolution_bitcast_fusion.3
  180.1 0.5 fusion.48
  180.7 0.0 copy-done.3
  180.7 0.4 fusion.74
  181.1 0.8 fusion.21
  181.9 0.1 copy.58
  182.1 46.9 %custom-call.18 = f32[8,64,64]{2,1,0:T(8,128)S(1)} custom-call(f32[8,64,64]{2,1,0:T(8,128)S(1)} %fusion.46), custom_call_target="Cholesky" | custom-call | tf_op jit(solution)/shard_map/jit(cholesky)/cholesky | solution.py:40
  229.0 0.1 compare_reduce_fusion.1
  229.1 0.1 select_bitcast_fusion.1
  229.2 39.3 %custom-call.20 = f32[8,1,64,64]{2,3,1,0:T(8,128)S(1)} custom-call(f32[8,1,64,64]{3,2,1,0:T(8,128)S(1)} %select_bitcast_fusion.1), custom_call_target="InvertDiagBlocksLowerTriangular" | custom-call | tf_op jit(solution)/shard_map/triangular_solve/custom-call.2 | solution.py:44
  268.6 0.0 copy-start.4
  268.6 2.4 fusion.65
  271.0 0.4 convolution_bitcast_fusion.2
  271.3 0.5 fusion.44
  271.8 0.0 copy-done.4
  271.9 0.4 fusion.72
  272.3 0.7 fusion.24
  273.0 0.1 copy.61
  273.2 47.1 %custom-call.21 = f32[8,64,64]{2,1,0:T(8,128)S(1)} custom-call(f32[8,64,64]{2,1,0:T(8,128)S(1)} %fusion.42), custom_call_target="Cholesky" | custom-call | tf_op jit(solution)/shard_map/jit(cholesky)/cholesky | solution.py:40
  320.4 0.1 compare_reduce_fusion
  320.5 0.1 select_bitcast_fusion
  320.6 39.3 %custom-call.23 = f32[8,1,64,64]{2,3,1,0:T(8,128)S(1)} custom-call(f32[8,1,64,64]{3,2,1,0:T(8,128)S(1)} %select_bitcast_fusion), custom_call_target="InvertDiagBlocksLowerTriangular" | custom-call | tf_op jit(solution)/shard_map/triangular_solve/custom-call.2 | solution.py:44
  359.9 2.2 fusion.63
  362.2 0.4 convolution_bitcast_fusion.1
  362.5 0.5 fusion.40
  363.1 0.6 add_bitcast_fusion
  (20 shorter events, 0.5 us)
Async XLA Ops:
  0.0 8.6 %copy-start = (bf16[1024,1024]{1,0:T(8,128)(2,1)S(1)}, bf16[1024,1024]{1,0:T(8,128)(2,1)}, u32[]{:S(2)}) copy-start(bf16[1024,1024]{1,0:T(8,128)(2,1)} %param.11) | copy-start | bytes 6291460
  0.0 3.6 copy-start.1
  4.8 3.2 copy-start.5
  8.6 6.3 %copy-start.6 = (f32[1,1024]{1,0:T(1,128)S(1)}, f32[1,1024]{1,0:T(1,128)}, u32[]{:S(2)}) copy-start(f32[1,1024]{1,0:T(1,128)} %param.12) | copy-start | bytes 12292
  8.6 6.3 %copy-start.7 = (f32[4]{0:T(128)S(1)}, f32[4]{0:T(128)}, u32[]{:S(2)}) copy-start(f32[4]{0:T(128)} %constant.65.clone) | copy-start | bytes 52
  31.6 54.3 %all-to-all-start = ((bf16[4,128,1,2048]{3,0,2,1:T(4,128)(2,1)}), bf16[4,128,1,2048]{3,0,2,1:T(4,128)(2,1)}, u32[]{:S(2)}, u32[]{:S(2)}) async-start(bf16[4,128,1,2048]{3,0,2,1:T(4,128)(2,1)} %copy.51), calls=%async_computation | async-start | bytes 4194304 | tf_op jit(solution)/shard_map/all_to_all | solution.py:78
  88.6 1.4 copy-start.2
  177.4 3.3 copy-start.3
  268.6 3.3 copy-start.4
where the time goes:
time: 364 us
  other arithmetic  273 us (75%)
  waiting for transfers between devices  47.1 us (13%)
  matrix products  25.4 us (7%)
  local copies, waits for them, and re-layouts  10.8 us (3%)
  starting transfers between devices  6.74 us (2%)
    another operation x10, other arithmetic, fit_traits(): factor = jnp.linalg.cholesky(gram + level_ridge * identity)  141 us
    another operation x7, other arithmetic, fit_traits(): lax.linalg.triangular_solve(factor, partial_solve, left_side=True, lower=...  118 us
    all_to_all x1, waiting for transfers between devices, on_device(): lax.all_to_all(predicted, 'region', split_axis=1, concat_axis=2, tiled=True)  47.1 us
    dot_general x1, matrix products, on_device(): lax.dot_general(ridge, std_geno, (((0,), (1,)), ((), ())), preferred_elem...  7.31 us
  transfers between devices with their start and end apart: 1, of which 1 were waited for; matrix products, arithmetic and copies ran while one was open for 0% of the time, Pallas kernels for 0%

commit v1 on v0

--- a/solution.py
+++ b/solution.py
@@ -75,7 +75,12 @@
         ridge, std_geno, (((0,), (1,)), ((), ())), preferred_element_type=jnp.float32
     ).astype(jnp.bfloat16)
     predicted = predicted.reshape(ridges, traits, 1, samples)
-    moved = lax.all_to_all(predicted, "region", split_axis=1, concat_axis=2, tiled=True)
+    moved = jnp.concatenate(
+        lax.all_to_all(
+            jnp.stack(jnp.split(predicted, lax.axis_size("region"), axis=1)), "region", 0, 0
+        ),
+        axis=2,
+    )
     target = lax.dynamic_slice_in_dim(pheno, position * per_device, per_device, 1)
     weights = fit_traits(moved, target.astype(jnp.float32).T, samples)
     return weights

time: 364 us -> 377 us (1.036)
  local copies, waits for them, and re-layouts: 10.8 us -> 24.1 us
    unnamed x17 -> x34, local copies, waits for them, and re-layouts: 1.67 us -> 18.9 us
    reshape x1 -> x0, local copies, waits for them, and re-layouts: 4.56 us -> none  [on_device(): predicted = predicted.reshape(ridges, traits, 1, samples)]
where the time goes in v1:
time: 377 us
  other arithmetic  273 us (72%)
  waiting for transfers between devices  47.1 us (12%)
  matrix products  25.4 us (7%)
  local copies, waits for them, and re-layouts  24.1 us (6%)
  starting transfers between devices  6.56 us (2%)
    another operation x10, other arithmetic, fit_traits(): factor = jnp.linalg.cholesky(gram + level_ridge * identity)  141 us
    another operation x7, other arithmetic, fit_traits(): lax.linalg.triangular_solve(factor, partial_solve, left_side=True, lower=...  118 us
    all_to_all x1, waiting for transfers between devices, on_device(): lax.all_to_all(jnp.stack(jnp.split(predicted, lax.axis_size('region'), ax...  47.1 us
    unnamed x34, local copies, waits for them, and re-layouts  18.9 us
  transfers between devices with their start and end apart: 1, of which 1 were waited for; matrix products, arithmetic and copies ran while one was open for 0% of the time, Pallas kernels for 0%

profile of v1, /device:TPU:13, one launch (start us, length us, event | category | flops | bytes accessed | tf_op | source)
XLA Modules:
  0.0 376.8 jit_solution(39605860104783510)
XLA Ops:
  0.0 3.0 convert_reduce_fusion
  3.1 0.5 copy-done.1
  3.6 1.1 fusion.2
  4.8 3.2 fusion.3
  8.0 0.3 convert_reduce_fusion.1
  8.3 0.3 fusion.27
  8.6 5.0 %convolution_bitcast_fusion = f32[1024,128]{0,1:T(8,128)} fusion(bf16[1024,1024]{1,0:T(8,128)(2,1)S(1)} %copy-done, bf16[2048,1024]{1,0:T(8,128)(2,1)} %fusion.3, bf16[2048,128]{1,0:T(8,128)(2,1)S(1)} %copy-done.5, f32[128]{0:T(128)S(1)} %add_sqrt_fusion.1, f32[128]{0:T(128)S(1)} %broadcast_multiply_fusion.1), kind=kOutput, calls=%fused_computation.25 | convolution fusion | flops 806486016 | bytes 7341056 | tf_op jit(solution)/shard_map/dot_general | solution.py:64
  13.6 1.2 copy.34
  14.9 0.2 broadcast_add_fusion
  15.1 4.6 %divide_convert_fusion = bf16[1024,4,128]{2,1,0:T(4,128)(2,1)} fusion(f32[1024,4]{1,0:T(8,128)S(1)} %broadcast_add_fusion, f32[1024,128]{1,0:T(8,128)S(1)} %copy.34), kind=kLoop, calls=%fused_computation.16 | loop fusion | flops 1048576 | bytes 1589248 | tf_op jit(solution)/shard_map/convert_element_type | solution.py:67
  19.7 7.3 %convolution_convert_fusion = bf16[512,2048]{1,0:T(8,128)(2,1)} fusion(bf16[2048,1024]{1,0:T(8,128)(2,1)} %fusion.3, bf16[1024,1024]{1,0:T(8,128)(2,1)S(1)} %copy-done, bf16[128,8,4,128]{3,2,1,0:T(4,128)(2,1)} %bitcast.288), kind=kOutput, calls=%fused_computation.15 | convolution fusion | flops 3222798336 | bytes 9437184 | tf_op jit(solution)/shard_map/dot_general | solution.py:74
  27.0 1.7 fusion.66
  28.7 1.6 fusion.65
  30.3 1.6 fusion.64
  31.8 1.6 fusion.63
  33.4 1.6 fusion.62
  34.9 1.6 fusion.61
  36.5 1.6 fusion.60
  38.1 1.6 fusion.59
  39.6 0.7 fusion.58
  40.3 0.7 fusion.57
  40.9 0.7 fusion.56
  41.6 0.7 fusion.55
  42.3 0.6 fusion.54
  42.9 0.7 fusion.53
  43.6 0.6 fusion.52
  44.2 0.7 fusion.51
  44.9 6.6 %all-to-all-start = ((bf16[16,4,8,1,2048]{4,2,1,3,0:T(8,128)(2,1)}), bf16[16,4,8,1,2048]{4,2,1,3,0:T(8,128)(2,1)}, u32[]{:S(2)}, u32[]{:S(2)}) async-start(bf16[16,4,8,1,2048]{4,2,1,3,0:T(8,128)(2,1)} %fusion.51), calls=%async_computation | async-start | bytes 4194304 | tf_op jit(solution)/shard_map/all_to_all | solution.py:79
  51.4 0.2 constant_dynamic-slice_fusion
  51.6 0.2 copy.73
  51.9 47.1 %all-to-all-done = bf16[16,4,8,1,2048]{4,2,1,3,0:T(8,128)(2,1)} async-done(((bf16[16,4,8,1,2048]{4,2,1,3,0:T(8,128)(2,1)}), bf16[16,4,8,1,2048]{4,2,1,3,0:T(8,128)(2,1)}, u32[]{:S(2)}, u32[]{:S(2)}) %all-to-all-start) | async-done | bytes 2097184 | tf_op jit(solution)/shard_map/all_to_all | solution.py:79
  99.0 2.7 copy.35
  101.7 0.4 fusion.92
  102.1 0.9 copy-done.2
  103.0 0.7 fusion.18
  103.8 0.1 copy.37
  104.0 46.9 %custom-call.15 = f32[8,64,64]{2,1,0:T(8,128)S(1)} custom-call(f32[8,64,64]{2,1,0:T(8,128)S(1)} %fusion.50), custom_call_target="Cholesky" | custom-call | tf_op jit(solution)/shard_map/jit(cholesky)/cholesky | solution.py:40
  150.9 0.1 compare_reduce_fusion.2
  151.0 0.1 select_bitcast_fusion.2
  151.2 39.3 %custom-call.17 = f32[8,1,64,64]{2,3,1,0:T(8,128)S(1)} custom-call(f32[8,1,64,64]{3,2,1,0:T(8,128)S(1)} %select_bitcast_fusion.2), custom_call_target="InvertDiagBlocksLowerTriangular" | custom-call | tf_op jit(solution)/shard_map/triangular_solve/custom-call.2 | solution.py:44
  190.5 2.4 convolution_bitcast_fusion.4
  192.9 0.4 convolution_bitcast_fusion.3
  193.2 0.5 fusion.48
  193.8 0.4 fusion.90
  194.2 0.8 fusion.21
  195.0 0.1 copy.41
  195.2 46.9 %custom-call.18 = f32[8,64,64]{2,1,0:T(8,128)S(1)} custom-call(f32[8,64,64]{2,1,0:T(8,128)S(1)} %fusion.46), custom_call_target="Cholesky" | custom-call | tf_op jit(solution)/shard_map/jit(cholesky)/cholesky | solution.py:40
  242.1 0.1 compare_reduce_fusion.1
  242.2 0.1 select_bitcast_fusion.1
  242.3 39.3 %custom-call.20 = f32[8,1,64,64]{2,3,1,0:T(8,128)S(1)} custom-call(f32[8,1,64,64]{3,2,1,0:T(8,128)S(1)} %select_bitcast_fusion.1), custom_call_target="InvertDiagBlocksLowerTriangular" | custom-call | tf_op jit(solution)/shard_map/triangular_solve/custom-call.2 | solution.py:44
  281.7 2.4 fusion.81
  284.1 0.4 convolution_bitcast_fusion.2
  284.4 0.5 fusion.44
  285.0 0.4 fusion.88
  285.4 0.7 fusion.24
  286.1 0.1 copy.44
  286.3 47.1 %custom-call.21 = f32[8,64,64]{2,1,0:T(8,128)S(1)} custom-call(f32[8,64,64]{2,1,0:T(8,128)S(1)} %fusion.42), custom_call_target="Cholesky" | custom-call | tf_op jit(solution)/shard_map/jit(cholesky)/cholesky | solution.py:40
  333.5 0.1 compare_reduce_fusion
  333.6 0.1 select_bitcast_fusion
  333.7 39.3 %custom-call.23 = f32[8,1,64,64]{2,3,1,0:T(8,128)S(1)} custom-call(f32[8,1,64,64]{3,2,1,0:T(8,128)S(1)} %select_bitcast_fusion), custom_call_target="InvertDiagBlocksLowerTriangular" | custom-call | tf_op jit(solution)/shard_map/triangular_solve/custom-call.2 | solution.py:44
  373.0 2.2 fusion.79
  375.3 0.4 convolution_bitcast_fusion.1
  375.6 0.5 fusion.40
  376.2 0.6 add_bitcast_fusion
  (36 shorter events, 0.5 us)
Async XLA Ops:
  0.0 8.6 %copy-start = (bf16[1024,1024]{1,0:T(8,128)(2,1)S(1)}, bf16[1024,1024]{1,0:T(8,128)(2,1)}, u32[]{:S(2)}) copy-start(bf16[1024,1024]{1,0:T(8,128)(2,1)} %param.11) | copy-start | bytes 6291460
  0.0 3.6 copy-start.1
  4.8 3.2 copy-start.5
  8.6 6.3 %copy-start.7 = (f32[1,1024]{1,0:T(1,128)S(1)}, f32[1,1024]{1,0:T(1,128)}, u32[]{:S(2)}) copy-start(f32[1,1024]{1,0:T(1,128)} %param.12) | copy-start | bytes 12292
  8.6 6.3 %copy-start.8 = (f32[4]{0:T(128)S(1)}, f32[4]{0:T(128)}, u32[]{:S(2)}) copy-start(f32[4]{0:T(128)} %constant.65.clone) | copy-start | bytes 52
  27.0 12.6 %copy-start.6 = (bf16[512,2048]{1,0:T(8,128)(2,1)S(1)}, bf16[512,2048]{1,0:T(8,128)(2,1)}, u32[]{:S(2)}) copy-start(bf16[512,2048]{1,0:T(8,128)(2,1)} %convolution_convert_fusion) | copy-start | bytes 6291460
  44.9 54.1 %all-to-all-start = ((bf16[16,4,8,1,2048]{4,2,1,3,0:T(8,128)(2,1)}), bf16[16,4,8,1,2048]{4,2,1,3,0:T(8,128)(2,1)}, u32[]{:S(2)}, u32[]{:S(2)}) async-start(bf16[16,4,8,1,2048]{4,2,1,3,0:T(8,128)(2,1)} %fusion.51), calls=%async_computation | async-start | bytes 4194304 | tf_op jit(solution)/shard_map/all_to_all | solution.py:79
  101.7 1.4 copy-start.2
  190.5 3.3 copy-start.3
  281.7 3.3 copy-start.4
